TPU v7x, 32 devices: a whole 2x2x4 slice. The times are simulated.
32 devices in a mesh: dp: 8 (over y, x, core), tensor: 4 (over z).
Axes of the slice: x: 2, y: 2, z: 4, core: 2. Of those that a mesh axis runs over, the one named last changes fastest.
Arguments:
- tokens: bfloat16 [16, 1024, 768], P('dp', 'tensor'), may hold values from -6 to 6
- segments: int32 [16, 1024], P('dp', 'tensor'), may hold values from 0 to 15, as said below
- cotangent: bfloat16 [16, 1024, 768], P('dp', 'tensor'), may hold values from -6 to 6
- w_qkv: bfloat16 [768, 3, 768], P('dp', None, 'tensor'), may hold values from -0.21875 to 0.21875
- w_out: bfloat16 [768, 768], P('tensor', 'dp'), may hold values from -3.5 to 3.5
- w_gate_up: bfloat16 [768, 2, 3072], P('dp', None, 'tensor'), may hold values from -0.21875 to 0.21875
- w_down: bfloat16 [3072, 768], P('tensor', 'dp'), may hold values from -0.109375 to 0.109375
- norm_gain: bfloat16 [2, 768], P(None, 'dp'), may hold values from 0.099609375 to 1.8984375
- norm_bias: bfloat16 [2, 768], P(None, 'dp'), may hold values from -3 to 3
Outputs:
- layer_out: bfloat16 [16, 1024, 768], P('dp', 'tensor')
- input_grad: bfloat16 [16, 1024, 768], P('dp', 'tensor')
- grad_qkv: float32 [768, 3, 768], P('dp', None, 'tensor')
- grad_out: float32 [768, 768], P('tensor', 'dp')
- grad_gate_up: float32 [768, 2, 3072], P('dp', None, 'tensor')
- grad_down: float32 [3072, 768], P('tensor', 'dp')
- grad_gain: float32 [2, 768], P(None, ('dp', 'tensor'))
- grad_bias: float32 [2, 768], P(None, ('dp', 'tensor'))
Inputs may be any that keep to these rules, and one draw needn't show every extreme that they name: `segments`: in each sequence the segment numbers start at 0 and never fall; every segment but a sequence's last holds 64 to 800 tokens; some sequence holds 16 documents.
All inputs are finite; a program needn't handle non-finite values.
Results may differ from a plain program's by a relative error of at most 0.025.
Values may be sent and summed in bfloat16 or wider, within the bound.
No kernel may reach another device: no remote copies, remote signals or barrier semaphores. Data moves between devices by JAX's collectives and lax.ppermute only.
A program may use at most 128 MiB of HBM per device.

v0:
```python
import jax
import jax.numpy as jnp
from jax import lax
from jax.sharding import PartitionSpec as P

HD = 64
rotary_base = 1000.0
norm_eps = 1e-06


def rotary_tables(segment_ids, head_size):
    length = segment_ids.shape[0]
    places = jnp.arange(length, dtype=jnp.int32)
    change = jnp.concatenate([jnp.ones((1,), dtype=jnp.bool_), segment_ids[1:] != segment_ids[:-1]])
    starts = lax.cummax(jnp.where(change, places, 0), axis=0)
    offsets = (places - starts).astype(jnp.float32)
    inverse_freq = rotary_base ** (-jnp.arange(0, head_size, 2, dtype=jnp.float32) / head_size)
    angles = offsets[:, None] * inverse_freq[None, :]
    return (jnp.cos(angles), jnp.sin(angles))


def rotate(values, cosine, sines):
    half_size = values.shape[-1] // 2
    front_half = values[..., :half_size]
    back_half = values[..., half_size:]
    cos_rows = cosine[:, None, :]
    sin_rows = sines[:, None, :]
    return jnp.concatenate(
        [
            front_half * cos_rows - back_half * sin_rows,
            back_half * cos_rows + front_half * sin_rows,
        ],
        axis=-1,
    )


def rotate_back(gradient, cosine, sines):
    half_size = gradient.shape[-1] // 2
    front_half = gradient[..., :half_size]
    back_half = gradient[..., half_size:]
    cos_rows = cosine[:, None, :]
    sin_rows = sines[:, None, :]
    return jnp.concatenate(
        [
            front_half * cos_rows + back_half * sin_rows,
            back_half * cos_rows - front_half * sin_rows,
        ],
        axis=-1,
    )


def norm_forward(inputs, gain_row, bias_row):
    center = inputs - jnp.mean(inputs, axis=-1, keepdims=True)
    inv_std = lax.rsqrt(jnp.mean(center * center, axis=-1, keepdims=True) + norm_eps)
    normed = center * inv_std
    return (normed * gain_row + bias_row, normed, inv_std)


def norm_backward(gradient, normed, inv_std, gain_row):
    scaled = gradient * gain_row
    mean_one = jnp.mean(scaled, axis=-1, keepdims=True)
    mean_two = jnp.mean(scaled * normed, axis=-1, keepdims=True)
    return (
        inv_std * (scaled - mean_one - normed * mean_two),
        jnp.sum(gradient * normed, axis=0),
        jnp.sum(gradient, axis=0),
    )


def contract_rows(left_side, right_side):
    return lax.dot_general(
        left_side, right_side, (((0,), (0,)), ((), ())), preferred_element_type=jnp.float32
    )


def contract_cols(left_side, right_side):
    return lax.dot_general(
        left_side, right_side, (((1,), (1,)), ((), ())), preferred_element_type=jnp.float32
    )


def block_scores(query_block, segment_block, key_all, segment_all, scale_factor):
    scores = (
        jnp.einsum("qhd,khd->hqk", query_block, key_all, preferred_element_type=jnp.float32)
        * scale_factor
    )
    same_doc = segment_block[:, None] == segment_all[None, :]
    return jnp.where(same_doc[None], scores, -1e30)


def per_device(tokens, segments, cotangent, w_qkv, w_out, w_gate_up, w_down, norm_gain, norm_bias):
    local_rows = tokens.shape[1]
    model_width = tokens.shape[2]
    seq_length = local_rows * lax.axis_size("tensor")
    local_width = w_qkv.shape[2]
    local_heads = local_width // HD
    local_hidden = w_gate_up.shape[2]
    scale_factor = HD ** (-0.5)
    block_rows = min(512, seq_length)
    block_count = seq_length // block_rows

    def micro_step(carry, batch_in):
        running, gain_sum, bias_sum = carry
        tokens_now, segments_now, cotangent_now = batch_in
        weight_set = (
            lax.all_gather(w_qkv, "dp", axis=0, tiled=True),
            lax.all_gather(w_out, "dp", axis=1, tiled=True),
            lax.all_gather(w_gate_up, "dp", axis=0, tiled=True),
            lax.all_gather(w_down, "dp", axis=1, tiled=True),
            lax.all_gather(norm_gain, "dp", axis=1, tiled=True),
            lax.all_gather(norm_bias, "dp", axis=1, tiled=True),
        )
        qkv_full, out_full, gate_up_full, down_full, gain_full, bias_full = weight_set
        gain_rows = gain_full.astype(jnp.float32)
        bias_rows = bias_full.astype(jnp.float32)
        qkv_flat = qkv_full.reshape(model_width, 3 * local_width)
        gate_up_flat = gate_up_full.reshape(model_width, 2 * local_hidden)
        rows_all, segment_all = (
            lax.all_gather(tokens_now, "tensor", axis=0, tiled=True),
            lax.all_gather(segments_now, "tensor", axis=0, tiled=True),
        )
        cosine, sines = rotary_tables(segment_all, HD)
        mixed = jnp.dot(rows_all, qkv_flat, preferred_element_type=jnp.float32).reshape(
            seq_length, 3, local_heads, HD
        )
        query_all = rotate(mixed[:, 0], cosine, sines).astype(jnp.bfloat16)
        key_all = rotate(mixed[:, 1], cosine, sines).astype(jnp.bfloat16)
        value_all = mixed[:, 2].astype(jnp.bfloat16)
        query_blocks = query_all.reshape(block_count, block_rows, local_heads, HD)
        segment_blocks = segment_all.reshape(block_count, block_rows)

        def attend(block_pair):
            masked = block_scores(block_pair[0], block_pair[1], key_all, segment_all, scale_factor)
            top_score = jnp.max(masked, axis=-1, keepdims=True)
            log_total = top_score + jnp.log(
                jnp.sum(jnp.exp(masked - top_score), axis=-1, keepdims=True)
            )
            attn_probs = jnp.exp(masked - log_total).astype(jnp.bfloat16)
            head_out = jnp.einsum(
                "hqk,khd->qhd", attn_probs, value_all, preferred_element_type=jnp.float32
            )
            return (head_out.astype(jnp.bfloat16), log_total[..., 0])

        heads_out, log_totals = lax.map(attend, (query_blocks, segment_blocks))
        joined = heads_out.reshape(seq_length, local_width)
        attn_rows = lax.psum_scatter(
            jnp.dot(joined, out_full, preferred_element_type=jnp.float32).astype(jnp.bfloat16),
            "tensor",
            scatter_dimension=0,
            tiled=True,
        ).astype(jnp.float32)
        first_out, first_normed, first_inv = norm_forward(
            tokens_now.astype(jnp.float32) + attn_rows, gain_rows[0], bias_rows[0]
        )
        first_all = lax.all_gather(first_out.astype(jnp.bfloat16), "tensor", axis=0, tiled=True)
        gate_up = jnp.dot(first_all, gate_up_flat, preferred_element_type=jnp.float32)
        gate_now = gate_up[:, :local_hidden]
        up_now = gate_up[:, local_hidden:]
        hidden = (jax.nn.silu(gate_now) * up_now).astype(jnp.bfloat16)
        branch_rows = lax.psum_scatter(
            jnp.dot(hidden, down_full, preferred_element_type=jnp.float32).astype(jnp.bfloat16),
            "tensor",
            scatter_dimension=0,
            tiled=True,
        ).astype(jnp.float32)
        second_out, second_normed, second_inv = norm_forward(
            first_out + branch_rows, gain_rows[1], bias_rows[1]
        )
        grad_second, gain_two, bias_two = norm_backward(
            cotangent_now.astype(jnp.float32), second_normed, second_inv, gain_rows[1]
        )
        branch_grad = lax.all_gather(grad_second.astype(jnp.bfloat16), "tensor", axis=0, tiled=True)
        down_grad = contract_rows(hidden, branch_grad)
        hidden_grad = contract_cols(branch_grad, down_full)
        sigmoid_gate = jax.nn.sigmoid(gate_now)
        gate_grad = hidden_grad * up_now * sigmoid_gate * (1.0 + gate_now * (1.0 - sigmoid_gate))
        up_grad = hidden_grad * gate_now * sigmoid_gate
        gate_up_grad = jnp.concatenate([gate_grad, up_grad], axis=1).astype(jnp.bfloat16)
        gate_up_wgrad = contract_rows(first_all, gate_up_grad)
        first_grad = grad_second + lax.psum_scatter(
            contract_cols(gate_up_grad, gate_up_flat).astype(jnp.bfloat16),
            "tensor",
            scatter_dimension=0,
            tiled=True,
        ).astype(jnp.float32)
        grad_first, gain_one, bias_one = norm_backward(
            first_grad, first_normed, first_inv, gain_rows[0]
        )
        attn_grad = lax.all_gather(grad_first.astype(jnp.bfloat16), "tensor", axis=0, tiled=True)
        out_wgrad = contract_rows(joined, attn_grad)
        joined_grad = contract_cols(attn_grad, out_full).astype(jnp.bfloat16)
        grad_blocks = joined_grad.reshape(block_count, block_rows, local_heads, HD)

        def attend_back(pair_sums, block_in):
            key_sum, value_sum = pair_sums
            query_block, segment_block, total_block, grad_block = block_in
            masked = block_scores(query_block, segment_block, key_all, segment_all, scale_factor)
            attn_probs = jnp.exp(masked - total_block[..., None])
            prob_grad = jnp.einsum(
                "qhd,khd->hqk", grad_block, value_all, preferred_element_type=jnp.float32
            )
            inner_sum = jnp.sum(attn_probs * prob_grad, axis=-1, keepdims=True)
            score_grad = (attn_probs * (prob_grad - inner_sum)).astype(jnp.bfloat16)
            query_grad = (
                jnp.einsum("hqk,khd->qhd", score_grad, key_all, preferred_element_type=jnp.float32)
                * scale_factor
            )
            key_sum = (
                key_sum
                + jnp.einsum(
                    "hqk,qhd->khd", score_grad, query_block, preferred_element_type=jnp.float32
                )
                * scale_factor
            )
            value_sum = value_sum + jnp.einsum(
                "hqk,qhd->khd",
                attn_probs.astype(jnp.bfloat16),
                grad_block,
                preferred_element_type=jnp.float32,
            )
            return ((key_sum, value_sum), query_grad)

        zero_grad = jnp.zeros((seq_length, local_heads, HD), jnp.float32)
        pair_out, query_grads = lax.scan(
            attend_back,
            (zero_grad, zero_grad),
            (query_blocks, segment_blocks, log_totals, grad_blocks),
        )
        key_grad, value_grad = pair_out
        query_grad_all = query_grads.reshape(seq_length, local_heads, HD)
        mixed_grad = jnp.stack(
            [
                rotate_back(query_grad_all, cosine, sines),
                rotate_back(key_grad, cosine, sines),
                value_grad,
            ],
            axis=1,
        )
        mixed_low = mixed_grad.reshape(seq_length, 3 * local_width).astype(jnp.bfloat16)
        qkv_wgrad = contract_rows(rows_all, mixed_low)
        input_now = (
            grad_first
            + lax.psum_scatter(
                contract_cols(mixed_low, qkv_flat).astype(jnp.bfloat16),
                "tensor",
                scatter_dimension=0,
                tiled=True,
            ).astype(jnp.float32)
        ).astype(jnp.bfloat16)
        step_grads = (
            qkv_wgrad.reshape(model_width, 3, local_width),
            out_wgrad,
            gate_up_wgrad.reshape(model_width, 2, local_hidden),
            down_grad,
        )
        running = tuple((before + added for before, added in zip(running, step_grads)))
        gain_sum = gain_sum + jnp.stack([gain_one, gain_two])
        bias_sum = bias_sum + jnp.stack([bias_one, bias_two])
        return ((running, gain_sum, bias_sum), (second_out.astype(jnp.bfloat16), input_now))

    start_sums = (
        jnp.zeros((model_width, 3, local_width), jnp.float32),
        jnp.zeros((local_width, model_width), jnp.float32),
        jnp.zeros((model_width, 2, local_hidden), jnp.float32),
        jnp.zeros((local_hidden, model_width), jnp.float32),
    )
    norm_zero = jnp.zeros((2, model_width), jnp.float32)
    carry_out, stacked = lax.scan(
        micro_step, (start_sums, norm_zero, norm_zero), (tokens, segments, cotangent)
    )
    weight_sums, gain_sum, bias_sum = carry_out
    layer_out, input_grads = stacked
    weight_sums = (
        lax.psum_scatter(weight_sums[0], "dp", scatter_dimension=0, tiled=True),
        lax.psum_scatter(weight_sums[1], "dp", scatter_dimension=1, tiled=True),
        lax.psum_scatter(weight_sums[2], "dp", scatter_dimension=0, tiled=True),
        lax.psum_scatter(weight_sums[3], "dp", scatter_dimension=1, tiled=True),
    )
    gain_grad, bias_grad = (
        lax.psum_scatter(gain_sum, ("dp", "tensor"), scatter_dimension=1, tiled=True),
        lax.psum_scatter(bias_sum, ("dp", "tensor"), scatter_dimension=1, tiled=True),
    )
    return (
        layer_out,
        input_grads,
        weight_sums[0],
        weight_sums[1],
        weight_sums[2],
        weight_sums[3],
        gain_grad,
        bias_grad,
    )


def solution(mesh):
    return jax.shard_map(
        per_device,
        mesh=mesh,
        in_specs=(
            P("dp", "tensor", None),
            P("dp", "tensor"),
            P("dp", "tensor", None),
            P("dp", None, "tensor"),
            P("tensor", "dp"),
            P("dp", None, "tensor"),
            P("tensor", "dp"),
            P(None, "dp"),
            P(None, "dp"),
        ),
        out_specs=(
            P("dp", "tensor", None),
            P("dp", "tensor", None),
            P("dp", None, "tensor"),
            P("tensor", "dp"),
            P("dp", None, "tensor"),
            P("tensor", "dp"),
            P(None, ("dp", "tensor")),
            P(None, ("dp", "tensor")),
        ),
        check_vma=False,
    )
```

profile of v0, /device:TPU:0, one launch (start us, length us, event | category | flops | bytes accessed | tf_op | source)
XLA Modules:
  0.0 1069.8 jit_solution(1454464533320853237)
XLA Ops:
  10.0 832.4 %while.56 = (s32[]{:T(128)}, f32[768,3,192]{0,2,1:T(8,128)}, f32[192,768]{1,0:T(8,128)}, f32[768,2,768]{2,1,0:T(2,128)}, f32[768,768]{1,0:T(8,128)}, /*index=5*/...) while((s32[]{:T(128)}, f32[768,3,192]{0,2,1:T(8,128)}, ...), condition=%wide.region_26.27_spmd.clone, body=%wide.region_0.26_spmd.clone.sunk | while | flops 16007278592 | bytes 422745888 | solution.py:268
  13.1 12.6 %all-gather.13 = s32[1,1024]{1,0:T(1,128)S(1)} all-gather(s32[1,256]{1,0:T(1,128)S(1)} %constant_dynamic-slice_fusion.12), channel_id=3, replica_groups=mesh['dp'=8,'tensor'=4] {'tensor'}, dimensions={1}, use_global_device_ids=true | all-gather | bytes 5120 | tf_op jit(solution)/shard_map/while/body/eval_jaxpr/all_gather | solution.py:120
  27.5 13.3 %all_gather.47 = bf16[768,3,192]{2,1,0:T(4,128)(2,1)S(1)} all-gather(bf16[96,3,192]{2,1,0:T(4,128)(2,1)S(1)} %get-tuple-element.1077), channel_id=1, replica_groups=mesh['dp'=8,'tensor'=4] {'dp'}, dimensions={0}, use_global_device_ids=true | all-gather | bytes 995328 | tf_op jit(solution)/shard_map/while/body/eval_jaxpr/all_gather | solution.py:106
  89.4 15.5 %reduce-scatter.18.cloned.1.call-done = bf16[256,768]{1,0:T(8,128)(2,1)} async-done(((bf16[1024,768]{1,0:T(8,128)(2,1)}), bf16[256,768]{1,0:T(8,128)(2,1)}) %reduce-scatter.18.cloned.1.call-update) | async-done | bytes 393232 | tf_op jit(solution)/shard_map/while/body/eval_jaxpr/reduce_scatter | solution.py:146
  113.8 31.3 %all-gather.25.cloned.1.call-done = bf16[1024,768]{1,0:T(8,128)(2,1)} async-done(((bf16[256,768]{1,0:T(8,128)(2,1)}), bf16[1024,768]{1,0:T(8,128)(2,1)}) %all-gather.25.cloned.1.call-update) | async-done | bytes 1572880 | tf_op jit(solution)/shard_map/while/body/eval_jaxpr/all_gather | solution.py:155
  154.5 15.1 %all-gather.29.cloned.1.call-done = bf16[768,768]{0,1:T(8,128)(2,1)} async-done(((bf16[768,96]{0,1:T(8,128)(2,1)}), bf16[768,768]{0,1:T(8,128)(2,1)}) %all-gather.29.cloned.1.call-update) | async-done | bytes 1179664 | tf_op jit(solution)/shard_map/while/body/eval_jaxpr/all_gather | solution.py:109
  174.0 35.5 %reduce-scatter.20.cloned.1.call-done = bf16[256,768]{1,0:T(8,128)(2,1)} async-done(((bf16[1024,768]{1,0:T(8,128)(2,1)}), bf16[256,768]{1,0:T(8,128)(2,1)}) %reduce-scatter.20.cloned.1.call-update) | async-done | bytes 393232 | tf_op jit(solution)/shard_map/while/body/eval_jaxpr/reduce_scatter | solution.py:160
  215.6 35.8 %all-gather.31.cloned.1.call-done = bf16[1024,768]{1,0:T(8,128)(2,1)} async-done(((bf16[256,768]{1,0:T(8,128)(2,1)}), bf16[1024,768]{1,0:T(8,128)(2,1)}) %all-gather.31.cloned.1.call-update) | async-done | bytes 1572880 | tf_op jit(solution)/shard_map/while/body/eval_jaxpr/all_gather | solution.py:172
  262.6 34.4 %reduce-scatter.22.cloned.1.call-done = bf16[256,768]{1,0:T(8,128)(2,1)} async-done(((bf16[1024,768]{1,0:T(8,128)(2,1)}), bf16[256,768]{1,0:T(8,128)(2,1)}) %reduce-scatter.22.cloned.1.call-update) | async-done | bytes 393232 | tf_op jit(solution)/shard_map/while/body/eval_jaxpr/reduce_scatter | solution.py:180
  304.5 33.4 %all-gather.33.cloned.1.call-done = bf16[1024,768]{1,0:T(8,128)(2,1)} async-done(((bf16[256,768]{1,0:T(8,128)(2,1)}), bf16[1024,768]{1,0:T(8,128)(2,1)}) %all-gather.33.cloned.1.call-update) | async-done | bytes 1572880 | tf_op jit(solution)/shard_map/while/body/eval_jaxpr/all_gather | solution.py:189
  342.0 40.5 %while.58 = (s32[]{:T(128)}, f32[1024,3,64]{0,2,1:T(8,128)S(1)}, f32[1024,3,64]{0,2,1:T(8,128)}, f32[2,512,3,64]{1,0,3,2:T(2,128)}, bf16[2,512,3,64]{1,3,2,0:T(8...) while((s32[]{:T(128)}, f32[1024,3,64]{0,2,1:T(8,128)S(1)}, ...), condition=%wide.region_20.20_spmd.clone, body=%wide.region_18.19_spmd.clone.sunk | while | flops 1031830016 | bytes 56418472 | solution.py:224
  440.5 13.2 %all_gather.47 = bf16[768,3,192]{2,1,0:T(4,128)(2,1)S(1)} all-gather(bf16[96,3,192]{2,1,0:T(4,128)(2,1)S(1)} %get-tuple-element.1077), channel_id=1, replica_groups=mesh['dp'=8,'tensor'=4] {'dp'}, dimensions={0}, use_global_device_ids=true | all-gather | bytes 995328 | tf_op jit(solution)/shard_map/while/body/eval_jaxpr/all_gather | solution.py:106
  502.2 15.3 %reduce-scatter.18.cloned.1.call-done = bf16[256,768]{1,0:T(8,128)(2,1)} async-done(((bf16[1024,768]{1,0:T(8,128)(2,1)}), bf16[256,768]{1,0:T(8,128)(2,1)}) %reduce-scatter.18.cloned.1.call-update) | async-done | bytes 393232 | tf_op jit(solution)/shard_map/while/body/eval_jaxpr/reduce_scatter | solution.py:146
  526.4 31.3 %all-gather.25.cloned.1.call-done = bf16[1024,768]{1,0:T(8,128)(2,1)} async-done(((bf16[256,768]{1,0:T(8,128)(2,1)}), bf16[1024,768]{1,0:T(8,128)(2,1)}) %all-gather.25.cloned.1.call-update) | async-done | bytes 1572880 | tf_op jit(solution)/shard_map/while/body/eval_jaxpr/all_gather | solution.py:155
  567.2 15.1 %all-gather.29.cloned.1.call-done = bf16[768,768]{0,1:T(8,128)(2,1)} async-done(((bf16[768,96]{0,1:T(8,128)(2,1)}), bf16[768,768]{0,1:T(8,128)(2,1)}) %all-gather.29.cloned.1.call-update) | async-done | bytes 1179664 | tf_op jit(solution)/shard_map/while/body/eval_jaxpr/all_gather | solution.py:109
  586.6 35.5 %reduce-scatter.20.cloned.1.call-done = bf16[256,768]{1,0:T(8,128)(2,1)} async-done(((bf16[1024,768]{1,0:T(8,128)(2,1)}), bf16[256,768]{1,0:T(8,128)(2,1)}) %reduce-scatter.20.cloned.1.call-update) | async-done | bytes 393232 | tf_op jit(solution)/shard_map/while/body/eval_jaxpr/reduce_scatter | solution.py:160
  628.2 35.8 %all-gather.31.cloned.1.call-done = bf16[1024,768]{1,0:T(8,128)(2,1)} async-done(((bf16[256,768]{1,0:T(8,128)(2,1)}), bf16[1024,768]{1,0:T(8,128)(2,1)}) %all-gather.31.cloned.1.call-update) | async-done | bytes 1572880 | tf_op jit(solution)/shard_map/while/body/eval_jaxpr/all_gather | solution.py:172
  675.2 34.5 %reduce-scatter.22.cloned.1.call-done = bf16[256,768]{1,0:T(8,128)(2,1)} async-done(((bf16[1024,768]{1,0:T(8,128)(2,1)}), bf16[256,768]{1,0:T(8,128)(2,1)}) %reduce-scatter.22.cloned.1.call-update) | async-done | bytes 393232 | tf_op jit(solution)/shard_map/while/body/eval_jaxpr/reduce_scatter | solution.py:180
  717.1 33.3 %all-gather.33.cloned.1.call-done = bf16[1024,768]{1,0:T(8,128)(2,1)} async-done(((bf16[256,768]{1,0:T(8,128)(2,1)}), bf16[1024,768]{1,0:T(8,128)(2,1)}) %all-gather.33.cloned.1.call-update) | async-done | bytes 1572880 | tf_op jit(solution)/shard_map/while/body/eval_jaxpr/all_gather | solution.py:189
  754.6 40.7 %while.58 = (s32[]{:T(128)}, f32[1024,3,64]{0,2,1:T(8,128)S(1)}, f32[1024,3,64]{0,2,1:T(8,128)}, f32[2,512,3,64]{1,0,3,2:T(2,128)}, bf16[2,512,3,64]{1,3,2,0:T(8...) while((s32[]{:T(128)}, f32[1024,3,64]{0,2,1:T(8,128)S(1)}, ...), condition=%wide.region_20.20_spmd.clone, body=%wide.region_18.19_spmd.clone.sunk | while | flops 1031830016 | bytes 56418472 | solution.py:224
  852.2 39.3 %all-reduce.3 = (f32[2,768]{1,0:T(2,128)S(1)}, f32[2,768]{1,0:T(2,128)S(1)}) all-reduce(f32[2,768]{1,0:T(2,128)S(1)} %copy-done.38, f32[2,768]{1,0:T(2,128)S(1)} %copy-done.35), channel_id=12, replica_groups=mesh['dp'=8,'tensor'=4] {'dp','tensor'}, use_global_device_ids=true, to_apply=%region_31.32.clone | all-reduce | flops 3072 | bytes 24576
  893.7 76.0 %all-reduce.6.cloned.1.call-done = f32[768,2,768]{2,1,0:T(2,128)} async-done(((f32[768,2,768]{2,1,0:T(2,128)}), f32[768,2,768]{2,1,0:T(2,128)}) %all-reduce.6.cloned.1.call-update) | async-done | bytes 4718608
  971.6 44.1 %reduce-scatter.12.cloned.1.call-done = f32[96,3,192]{2,0,1:T(8,128)} async-done(((f32[768,3,192]{2,0,1:T(8,128)}), f32[96,3,192]{2,0,1:T(8,128)}) %reduce-scatter.12.cloned.1.call-update) | async-done | bytes 221200 | tf_op jit(solution)/shard_map/reduce_scatter | solution.py:274
  1015.8 46.1 %reduce-scatter.14.cloned.1.call-done = f32[768,96]{0,1:T(8,128)} async-done(((f32[768,768]{0,1:T(8,128)}), f32[768,96]{0,1:T(8,128)}) %reduce-scatter.14.cloned.1.call-update) | async-done | bytes 294928 | tf_op jit(solution)/shard_map/reduce_scatter | solution.py:277
  (513 shorter events, 425.4 us)
Async XLA Ops:
  10.5 42.1 %all-gather.23.cloned.1.call-start = ((), (), s32[]{:S(2)}) async-start(), calls=%async_computation.11 | async-start | bytes 1966080 | tf_op jit(solution)/shard_map/while/body/eval_jaxpr/all_gather | solution.py:119
  12.4 92.5 %reduce-scatter.18.cloned.1.call-start = ((), (), s32[]{:S(2)}) async-start(), calls=%async_computation.12 | async-start | bytes 1966080 | tf_op jit(solution)/shard_map/while/body/eval_jaxpr/reduce_scatter | solution.py:146
  70.3 39.8 %all-gather.27.cloned.1.call-start = ((), (), s32[]{:S(2)}) async-start(), calls=%async_computation.14 | async-start | bytes 2654208 | tf_op jit(solution)/shard_map/while/body/eval_jaxpr/all_gather | solution.py:108
  70.9 74.2 %all-gather.25.cloned.1.call-start = ((), (), s32[]{:S(2)}) async-start(), calls=%async_computation.13 | async-start | bytes 1966080 | tf_op jit(solution)/shard_map/while/body/eval_jaxpr/all_gather | solution.py:155
  109.3 60.3 %all-gather.29.cloned.1.call-start = ((), (), s32[]{:S(2)}) async-start(), calls=%async_computation.15 | async-start | bytes 1327104 | tf_op jit(solution)/shard_map/while/body/eval_jaxpr/all_gather | solution.py:109
  109.9 99.6 %reduce-scatter.20.cloned.1.call-start = ((), (), s32[]{:S(2)}) async-start(), calls=%async_computation.16 | async-start | bytes 1966080 | tf_op jit(solution)/shard_map/while/body/eval_jaxpr/reduce_scatter | solution.py:160
  173.9 77.4 %all-gather.31.cloned.1.call-start = ((), (), s32[]{:S(2)}) async-start(), calls=%async_computation.17 | async-start | bytes 1966080 | tf_op jit(solution)/shard_map/while/body/eval_jaxpr/all_gather | solution.py:172
  215.5 81.6 %reduce-scatter.22.cloned.1.call-start = ((), (), s32[]{:S(2)}) async-start(), calls=%async_computation.18 | async-start | bytes 1966080 | tf_op jit(solution)/shard_map/while/body/eval_jaxpr/reduce_scatter | solution.py:180
  262.6 75.3 %all-gather.33.cloned.1.call-start = ((), (), s32[]{:S(2)}) async-start(), calls=%async_computation.19 | async-start | bytes 1966080 | tf_op jit(solution)/shard_map/while/body/eval_jaxpr/all_gather | solution.py:189
  302.0 123.1 %reduce-scatter.24.cloned.1.call-start = ((), (), s32[]{:S(2)}) async-start(), calls=%async_computation.20 | async-start | bytes 1966080 | tf_op jit(solution)/shard_map/while/body/eval_jaxpr/reduce_scatter | solution.py:243
  427.3 38.0 %all-gather.23.cloned.1.call-start = ((), (), s32[]{:S(2)}) async-start(), calls=%async_computation.11 | async-start | bytes 1966080 | tf_op jit(solution)/shard_map/while/body/eval_jaxpr/all_gather | solution.py:119
  429.2 88.3 %reduce-scatter.18.cloned.1.call-start = ((), (), s32[]{:S(2)}) async-start(), calls=%async_computation.12 | async-start | bytes 1966080 | tf_op jit(solution)/shard_map/while/body/eval_jaxpr/reduce_scatter | solution.py:146
  483.0 39.8 %all-gather.27.cloned.1.call-start = ((), (), s32[]{:S(2)}) async-start(), calls=%async_computation.14 | async-start | bytes 2654208 | tf_op jit(solution)/shard_map/while/body/eval_jaxpr/all_gather | solution.py:108
  483.7 74.0 %all-gather.25.cloned.1.call-start = ((), (), s32[]{:S(2)}) async-start(), calls=%async_computation.13 | async-start | bytes 1966080 | tf_op jit(solution)/shard_map/while/body/eval_jaxpr/all_gather | solution.py:155
  521.9 60.3 %all-gather.29.cloned.1.call-start = ((), (), s32[]{:S(2)}) async-start(), calls=%async_computation.15 | async-start | bytes 1327104 | tf_op jit(solution)/shard_map/while/body/eval_jaxpr/all_gather | solution.py:109
  522.5 99.6 %reduce-scatter.20.cloned.1.call-start = ((), (), s32[]{:S(2)}) async-start(), calls=%async_computation.16 | async-start | bytes 1966080 | tf_op jit(solution)/shard_map/while/body/eval_jaxpr/reduce_scatter | solution.py:160
  586.6 77.4 %all-gather.31.cloned.1.call-start = ((), (), s32[]{:S(2)}) async-start(), calls=%async_computation.17 | async-start | bytes 1966080 | tf_op jit(solution)/shard_map/while/body/eval_jaxpr/all_gather | solution.py:172
  628.1 81.6 %reduce-scatter.22.cloned.1.call-start = ((), (), s32[]{:S(2)}) async-start(), calls=%async_computation.18 | async-start | bytes 1966080 | tf_op jit(solution)/shard_map/while/body/eval_jaxpr/reduce_scatter | solution.py:180
  675.2 75.3 %all-gather.33.cloned.1.call-start = ((), (), s32[]{:S(2)}) async-start(), calls=%async_computation.19 | async-start | bytes 1966080 | tf_op jit(solution)/shard_map/while/body/eval_jaxpr/all_gather | solution.py:189
  714.7 123.3 %reduce-scatter.24.cloned.1.call-start = ((), (), s32[]{:S(2)}) async-start(), calls=%async_computation.20 | async-start | bytes 1966080 | tf_op jit(solution)/shard_map/while/body/eval_jaxpr/reduce_scatter | solution.py:243
  842.5 49.6 %reduce-scatter.16.cloned.1.call-start = ((), (), s32[]{:S(2)}) async-start(), calls=%async_computation.9 | async-start | bytes 884736
  844.8 124.9 %all-reduce.6.cloned.1.call-start = ((), (), s32[]{:S(2)}) async-start(), calls=%async_computation.10 | async-start | bytes 9437184
  845.5 170.2 %reduce-scatter.12.cloned.1.call-start = ((), (), s32[]{:S(2)}) async-start(), calls=%async_computation.7 | async-start | bytes 2654208 | tf_op jit(solution)/shard_map/reduce_scatter | solution.py:274
  848.8 213.1 %reduce-scatter.14.cloned.1.call-start = ((), (), s32[]{:S(2)}) async-start(), calls=%async_computation.8 | async-start | bytes 2654208 | tf_op jit(solution)/shard_map/reduce_scatter | solution.py:277
  (100 other events, 899.1 us)
Sparse Core Ops, SparseCore 0:
  12.9 39.7 all-gather.22
  70.5 34.3 reduce-scatter.17
  174.1 35.4 reduce-scatter.19
  262.7 34.3 reduce-scatter.21
  390.8 34.3 reduce-scatter.23
  429.4 35.8 all-gather.22
  483.1 34.2 reduce-scatter.17
  586.7 35.4 reduce-scatter.19
  675.3 34.3 reduce-scatter.21
  803.6 34.3 reduce-scatter.23
Sparse Core Ops, SparseCore 1:
  72.7 27.6 all-gather.26
  109.4 35.6 all-gather.24
  146.9 22.7 all-gather.28
  215.6 35.7 all-gather.30
  302.1 35.7 all-gather.32
  485.7 27.6 all-gather.26
  522.0 35.6 all-gather.24
  559.5 22.7 all-gather.28
  628.2 35.7 all-gather.30
  714.8 35.6 all-gather.32
  846.1 33.8 reduce-scatter.15
  883.3 86.3 all-reduce.5
  973.5 42.2 reduce-scatter.11
  1019.7 42.1 reduce-scatter.13
where the time goes:
time: 1080 us; the launch traced here: 1070 us
  waiting for transfers between devices  583 us (54%)
  blocking collectives  139 us (13%)
  matrix products  133 us (12%)
  local copies, waits for them, and re-layouts  108 us (10%)
  other arithmetic  81.5 us (8%)
  between operations  16.7 us (2%)
    unnamed x6, waiting for transfers between devices  76.7 us
    all_gather x2, waiting for transfers between devices, micro_step(): lax.all_gather(grad_second.astype(jnp.bfloat16), 'tensor', axis=0, tiled=...  71.5 us
    reduce_scatter x2, waiting for transfers between devices, micro_step(): lax.psum_scatter(jnp.dot(hidden, down_full, preferred_element_type=jnp.fl...  71.1 us
    reduce_scatter x2, waiting for transfers between devices, micro_step(): lax.psum_scatter(contract_cols(gate_up_grad, gate_up_flat).astype(jnp.bfl...  68.9 us
    all_gather x2, waiting for transfers between devices, micro_step(): lax.all_gather(grad_first.astype(jnp.bfloat16), 'tensor', axis=0, tiled=T...  66.7 us
    all_gather x2, waiting for transfers between devices, micro_step(): lax.all_gather(first_out.astype(jnp.bfloat16), 'tensor', axis=0, tiled=True)  62.6 us
    reduce_scatter x1, waiting for transfers between devices, per_device(): lax.psum_scatter(weight_sums[3], 'dp', scatter_dimension=1, tiled=True)  46.1 us
    reduce_scatter x1, waiting for transfers between devices, per_device(): lax.psum_scatter(weight_sums[0], 'dp', scatter_dimension=0, tiled=True)  44.1 us
  transfers between devices with their start and end apart: 24, of which 21 were waited for; matrix products, arithmetic and copies ran while one was open for 10% of the time, Pallas kernels for 0%

commit v1 on v0

--- a/solution.py
+++ b/solution.py
@@ -6,6 +6,12 @@
 HD = 64
 rotary_base = 1000.0
 norm_eps = 1e-06
+
+
+def in_order(pieces, dim):
+    dims = list(pieces.shape[1:])
+    dims[dim] *= pieces.shape[0]
+    return jnp.moveaxis(pieces, 0, dim).reshape(dims)
 
 
 def rotary_tables(segment_ids, head_size):
@@ -152,7 +158,20 @@
         first_out, first_normed, first_inv = norm_forward(
             tokens_now.astype(jnp.float32) + attn_rows, gain_rows[0], bias_rows[0]
         )
-        first_all = lax.all_gather(first_out.astype(jnp.bfloat16), "tensor", axis=0, tiled=True)
+        shard = first_out.astype(jnp.bfloat16)
+        devices = lax.axis_size("tensor")
+        pairs = [(i, (i + 1) % devices) for i in range(devices)]
+        back = [(b, a) for a, b in pairs]
+        lower, upper = ([], [])
+        for lap in range(devices - 1):
+            if lap % 2 == 0:
+                lower.append(lax.ppermute(lower[-1] if lower else shard, "tensor", pairs))
+            else:
+                upper.append(lax.ppermute(upper[-1] if upper else shard, "tensor", back))
+        blocks = jnp.stack([*lower[::-1], shard, *upper])
+        shift = lax.axis_index("tensor") - len(lower)
+        blocks = blocks[(jnp.arange(devices) - shift) % devices]
+        first_all = in_order(blocks, 0)
         gate_up = jnp.dot(first_all, gate_up_flat, preferred_element_type=jnp.float32)
         gate_now = gate_up[:, :local_hidden]
         up_now = gate_up[:, local_hidden:]

time: 1080 us -> 1040 us (0.963)
  waiting for transfers between devices: 583 us -> 533 us
  starting transfers between devices: 1.44 us -> 16.8 us
    all_gather x2 -> x0, waiting for transfers between devices: 62.6 us -> none  [micro_step(): lax.all_gather(first_out.astype(jnp.bfloat16), 'tensor', axis=0, tiled=True)]
    ppermute x0 -> x6, waiting for transfers between devices: none -> 34 us  [the longest x4 34 us: micro_step(): lower.append(lax.ppermute(lower[-1] if lower else shard, 'tensor', pairs))]
    all_gather x2, waiting for transfers between devices: 30.1 us -> 0.05 us  [micro_step(): lax.all_gather(w_down, 'dp', axis=1, tiled=True)]
    reduce_scatter x2, waiting for transfers between devices: 8.55 us -> 24.5 us  [micro_step(): lax.psum_scatter(contract_cols(mixed_low, qkv_flat).astype(jnp.bfloat16),...]
    ppermute x0 -> x6, starting transfers between devices: none -> 15.8 us  [the longest x4 8.35 us: micro_step(): lower.append(lax.ppermute(lower[-1] if lower else shard, 'tensor', pairs))]
    reshape x2 -> x0, local copies, waits for them, and re-layouts: 14 us -> none  [micro_step(): gate_up_wgrad.reshape(model_width, 2, local_hidden)]
    add x2 -> x0, other arithmetic: 13.1 us -> none  [micro_step(): before + added]
    while x200 -> x244, local copies, waits for them, and re-layouts: 24.6 us -> 28.6 us
  transfers between devices with their start and end apart: 24 -> 28, of which waited for: 21 -> 21; matrix products, arithmetic and copies ran while one was open for 10% -> 10% of each run, Pallas kernels for 0% -> 0%
where the time goes in v1:
time: 1040 us
  waiting for transfers between devices  533 us (51%)
  blocking collectives  140 us (13%)
  matrix products  132 us (13%)
  local copies, waits for them, and re-layouts  117 us (11%)
  other arithmetic  72.8 us (7%)
  starting transfers between devices  16.8 us (2%)
  between operations  16.3 us (2%)
    all_gather x2, waiting for transfers between devices, micro_step(): lax.all_gather(grad_second.astype(jnp.bfloat16), 'tensor', axis=0, tiled=...  72 us
    all_gather x2, waiting for transfers between devices, micro_step(): lax.all_gather(grad_first.astype(jnp.bfloat16), 'tensor', axis=0, tiled=T...  71.9 us
    unnamed x6, waiting for transfers between devices  69 us
    reduce_scatter x2, waiting for transfers between devices, micro_step(): lax.psum_scatter(contract_cols(gate_up_grad, gate_up_flat).astype(jnp.bfl...  68.8 us
    reduce_scatter x2, waiting for transfers between devices, micro_step(): lax.psum_scatter(jnp.dot(hidden, down_full, preferred_element_type=jnp.fl...  67.3 us
    reduce_scatter x1, waiting for transfers between devices, per_device(): lax.psum_scatter(weight_sums[3], 'dp', scatter_dimension=1, tiled=True)  46 us
    reduce_scatter x1, waiting for transfers between devices, per_device(): lax.psum_scatter(weight_sums[0], 'dp', scatter_dimension=0, tiled=True)  44.1 us
    unnamed x1, blocking collectives  39.8 us
  transfers between devices with their start and end apart: 28, of which 21 were waited for; matrix products, arithmetic and copies ran while one was open for 10% of the time, Pallas kernels for 0%

profile of v1, /device:TPU:0, one launch (start us, length us, event | category | flops | bytes accessed | tf_op | source)
XLA Modules:
  0.0 1036.6 jit_solution(15839199164411913068)
XLA Ops:
  10.0 799.0 %while.85 = (s32[]{:T(128)}, f32[768,3,192]{0,2,1:T(8,128)}, f32[192,768]{1,0:T(8,128)}, f32[768,2,768]{2,0,1:T(8,128)}, f32[768,768]{1,0:T(8,128)}, /*index=5*/...) while((s32[]{:T(128)}, f32[768,3,192]{0,2,1:T(8,128)}, ...), condition=%wide.region_26.27_spmd.clone, body=%wide.region_0.26_spmd.clone.sunk | while | flops 16009639936 | bytes 422430912 | solution.py:287
  13.1 12.6 %all-gather.13 = s32[1,1024]{1,0:T(1,128)S(1)} all-gather(s32[1,256]{1,0:T(1,128)S(1)} %constant_dynamic-slice_fusion.12), channel_id=3, replica_groups=mesh['dp'=8,'tensor'=4] {'tensor'}, dimensions={1}, use_global_device_ids=true | all-gather | bytes 5120 | tf_op jit(solution)/shard_map/while/body/eval_jaxpr/all_gather | solution.py:126
  27.5 13.3 %all_gather.72 = bf16[768,3,192]{2,1,0:T(4,128)(2,1)S(1)} all-gather(bf16[96,3,192]{2,1,0:T(4,128)(2,1)S(1)} %get-tuple-element.1212), channel_id=1, replica_groups=mesh['dp'=8,'tensor'=4] {'dp'}, dimensions={0}, use_global_device_ids=true | all-gather | bytes 995328 | tf_op jit(solution)/shard_map/while/body/eval_jaxpr/all_gather | solution.py:112
  55.7 12.7 %while.86 = (s32[]{:T(128)}, bf16[2,512,3,64]{1,3,2,0:T(8,128)(2,1)}, f32[2,3,512]{2,1,0:T(4,128)S(1)}, s32[2,512]{1,0:T(2,128)S(1)}, s32[1024]{0:T(1024)S(1)}, ...) while((s32[]{:T(128)}, ...), condition=%wide.region_6.6_spmd, body=%wide.region_3.5_spmd.sunk | while | flops 420575744 | bytes 25366700 | solution.py:150
  91.6 15.5 %reduce-scatter.18.cloned.1.call-done = bf16[256,768]{1,0:T(8,128)(2,1)} async-done(((bf16[1024,768]{1,0:T(8,128)(2,1)}), bf16[256,768]{1,0:T(8,128)(2,1)}) %reduce-scatter.18.cloned.1.call-update) | async-done | bytes 393232 | tf_op jit(solution)/shard_map/while/body/eval_jaxpr/reduce_scatter | solution.py:152
  158.2 33.7 %reduce-scatter.20.cloned.1.call-done = bf16[256,768]{1,0:T(8,128)(2,1)} async-done(((bf16[1024,768]{1,0:T(8,128)(2,1)}), bf16[256,768]{1,0:T(8,128)(2,1)}) %reduce-scatter.20.cloned.1.call-update) | async-done | bytes 393232 | tf_op jit(solution)/shard_map/while/body/eval_jaxpr/reduce_scatter | solution.py:179
  197.9 36.0 %all-gather.28.cloned.1.call-done = bf16[1024,768]{1,0:T(8,128)(2,1)} async-done(((bf16[256,768]{1,0:T(8,128)(2,1)}), bf16[1024,768]{1,0:T(8,128)(2,1)}) %all-gather.28.cloned.1.call-update) | async-done | bytes 1572880 | tf_op jit(solution)/shard_map/while/body/eval_jaxpr/all_gather | solution.py:191
  245.2 34.4 %reduce-scatter.22.cloned.1.call-done = bf16[256,768]{1,0:T(8,128)(2,1)} async-done(((bf16[1024,768]{1,0:T(8,128)(2,1)}), bf16[256,768]{1,0:T(8,128)(2,1)}) %reduce-scatter.22.cloned.1.call-update) | async-done | bytes 393232 | tf_op jit(solution)/shard_map/while/body/eval_jaxpr/reduce_scatter | solution.py:199
  284.7 36.0 %all-gather.30.cloned.1.call-done = bf16[1024,768]{1,0:T(8,128)(2,1)} async-done(((bf16[256,768]{1,0:T(8,128)(2,1)}), bf16[1024,768]{1,0:T(8,128)(2,1)}) %all-gather.30.cloned.1.call-update) | async-done | bytes 1572880 | tf_op jit(solution)/shard_map/while/body/eval_jaxpr/all_gather | solution.py:208
  324.8 40.6 %while.87 = (s32[]{:T(128)}, f32[1024,3,64]{0,2,1:T(8,128)S(1)}, f32[1024,3,64]{0,2,1:T(8,128)}, f32[2,512,3,64]{1,0,3,2:T(2,128)}, bf16[2,512,3,64]{1,3,2,0:T(8...) while((s32[]{:T(128)}, f32[1024,3,64]{0,2,1:T(8,128)S(1)}, ...), condition=%wide.region_20.20_spmd.clone, body=%wide.region_18.19_spmd.clone.sunk | while | flops 1031830016 | bytes 56418472 | solution.py:243
  392.9 14.2 %reduce-scatter.24.cloned.1.call-done = bf16[256,768]{1,0:T(8,128)(2,1)} async-done(((bf16[1024,768]{1,0:T(8,128)(2,1)}), bf16[256,768]{1,0:T(8,128)(2,1)}) %reduce-scatter.24.cloned.1.call-update) | async-done | bytes 393232 | tf_op jit(solution)/shard_map/while/body/eval_jaxpr/reduce_scatter | solution.py:262
  422.4 13.2 %all_gather.72 = bf16[768,3,192]{2,1,0:T(4,128)(2,1)S(1)} all-gather(bf16[96,3,192]{2,1,0:T(4,128)(2,1)S(1)} %get-tuple-element.1212), channel_id=1, replica_groups=mesh['dp'=8,'tensor'=4] {'dp'}, dimensions={0}, use_global_device_ids=true | all-gather | bytes 995328 | tf_op jit(solution)/shard_map/while/body/eval_jaxpr/all_gather | solution.py:112
  450.6 12.7 %while.86 = (s32[]{:T(128)}, bf16[2,512,3,64]{1,3,2,0:T(8,128)(2,1)}, f32[2,3,512]{2,1,0:T(4,128)S(1)}, s32[2,512]{1,0:T(2,128)S(1)}, s32[1024]{0:T(1024)S(1)}, ...) while((s32[]{:T(128)}, ...), condition=%wide.region_6.6_spmd, body=%wide.region_3.5_spmd.sunk | while | flops 420575744 | bytes 25366700 | solution.py:150
  486.5 15.4 %reduce-scatter.18.cloned.1.call-done = bf16[256,768]{1,0:T(8,128)(2,1)} async-done(((bf16[1024,768]{1,0:T(8,128)(2,1)}), bf16[256,768]{1,0:T(8,128)(2,1)}) %reduce-scatter.18.cloned.1.call-update) | async-done | bytes 393232 | tf_op jit(solution)/shard_map/while/body/eval_jaxpr/reduce_scatter | solution.py:152
  553.0 33.7 %reduce-scatter.20.cloned.1.call-done = bf16[256,768]{1,0:T(8,128)(2,1)} async-done(((bf16[1024,768]{1,0:T(8,128)(2,1)}), bf16[256,768]{1,0:T(8,128)(2,1)}) %reduce-scatter.20.cloned.1.call-update) | async-done | bytes 393232 | tf_op jit(solution)/shard_map/while/body/eval_jaxpr/reduce_scatter | solution.py:179
  592.7 36.0 %all-gather.28.cloned.1.call-done = bf16[1024,768]{1,0:T(8,128)(2,1)} async-done(((bf16[256,768]{1,0:T(8,128)(2,1)}), bf16[1024,768]{1,0:T(8,128)(2,1)}) %all-gather.28.cloned.1.call-update) | async-done | bytes 1572880 | tf_op jit(solution)/shard_map/while/body/eval_jaxpr/all_gather | solution.py:191
  640.0 34.4 %reduce-scatter.22.cloned.1.call-done = bf16[256,768]{1,0:T(8,128)(2,1)} async-done(((bf16[1024,768]{1,0:T(8,128)(2,1)}), bf16[256,768]{1,0:T(8,128)(2,1)}) %reduce-scatter.22.cloned.1.call-update) | async-done | bytes 393232 | tf_op jit(solution)/shard_map/while/body/eval_jaxpr/reduce_scatter | solution.py:199
  679.5 36.0 %all-gather.30.cloned.1.call-done = bf16[1024,768]{1,0:T(8,128)(2,1)} async-done(((bf16[256,768]{1,0:T(8,128)(2,1)}), bf16[1024,768]{1,0:T(8,128)(2,1)}) %all-gather.30.cloned.1.call-update) | async-done | bytes 1572880 | tf_op jit(solution)/shard_map/while/body/eval_jaxpr/all_gather | solution.py:208
  719.7 40.8 %while.87 = (s32[]{:T(128)}, f32[1024,3,64]{0,2,1:T(8,128)S(1)}, f32[1024,3,64]{0,2,1:T(8,128)}, f32[2,512,3,64]{1,0,3,2:T(2,128)}, bf16[2,512,3,64]{1,3,2,0:T(8...) while((s32[]{:T(128)}, f32[1024,3,64]{0,2,1:T(8,128)S(1)}, ...), condition=%wide.region_20.20_spmd.clone, body=%wide.region_18.19_spmd.clone.sunk | while | flops 1031830016 | bytes 56418472 | solution.py:243
  791.8 10.3 reduce-scatter.24.cloned.1.call-done
  826.1 39.8 %all-reduce.3 = (f32[2,768]{1,0:T(2,128)S(1)}, f32[2,768]{1,0:T(2,128)S(1)}) all-reduce(f32[2,768]{1,0:T(2,128)S(1)} %copy-done.54, f32[2,768]{1,0:T(2,128)S(1)} %copy-done.51), channel_id=12, replica_groups=mesh['dp'=8,'tensor'=4] {'dp','tensor'}, use_global_device_ids=true, to_apply=%region_31.32.clone | all-reduce | flops 3072 | bytes 24576
  868.2 68.9 %all-reduce.6.cloned.1.call-done = f32[768,2,768]{2,1,0:T(2,128)} async-done(((f32[768,2,768]{2,1,0:T(2,128)}), f32[768,2,768]{2,1,0:T(2,128)}) %all-reduce.6.cloned.1.call-update) | async-done | bytes 4718608
  939.1 44.1 %reduce-scatter.12.cloned.1.call-done = f32[96,3,192]{2,0,1:T(8,128)} async-done(((f32[768,3,192]{2,0,1:T(8,128)}), f32[96,3,192]{2,0,1:T(8,128)}) %reduce-scatter.12.cloned.1.call-update) | async-done | bytes 221200 | tf_op jit(solution)/shard_map/reduce_scatter | solution.py:293
  983.2 46.0 %reduce-scatter.14.cloned.1.call-done = f32[768,96]{0,1:T(8,128)} async-done(((f32[768,768]{0,1:T(8,128)}), f32[768,96]{0,1:T(8,128)}) %reduce-scatter.14.cloned.1.call-update) | async-done | bytes 294928 | tf_op jit(solution)/shard_map/reduce_scatter | solution.py:296
  (570 shorter events, 438.5 us)
Async XLA Ops:
  10.5 42.1 %all-gather.22.cloned.1.call-start = ((), (), s32[]{:S(2)}) async-start(), calls=%async_computation.11 | async-start | bytes 1966080 | tf_op jit(solution)/shard_map/while/body/eval_jaxpr/all_gather | solution.py:125
  12.4 94.7 %reduce-scatter.18.cloned.1.call-start = ((), (), s32[]{:S(2)}) async-start(), calls=%async_computation.12 | async-start | bytes 1966080 | tf_op jit(solution)/shard_map/while/body/eval_jaxpr/reduce_scatter | solution.py:152
  72.6 56.6 %all-gather.24.cloned.1.call-start = ((), (), s32[]{:S(2)}) async-start(), calls=%async_computation.13 | async-start | bytes 2654208 | tf_op jit(solution)/shard_map/while/body/eval_jaxpr/all_gather | solution.py:114
  73.1 80.6 %all-gather.26.cloned.1.call-start = ((), (), s32[]{:S(2)}) async-start(), calls=%async_computation.14 | async-start | bytes 1327104 | tf_op jit(solution)/shard_map/while/body/eval_jaxpr/all_gather | solution.py:115
  111.0 80.8 %reduce-scatter.20.cloned.1.call-start = ((), (), s32[]{:S(2)}) async-start(), calls=%async_computation.15 | async-start | bytes 1966080 | tf_op jit(solution)/shard_map/while/body/eval_jaxpr/reduce_scatter | solution.py:179
  111.1 21.7 %collective-permute-start = (bf16[256,768]{1,0:T(8,128)(2,1)S(1)}, bf16[256,768]{1,0:T(8,128)(2,1)S(1)}, u32[]{:S(2)}, u32[]{:S(2)}) collective-permute-start(bf16[256,768]{1,0:T(8,128)(2,1)S(1)} %fusion.188), channel_id=1, source_target_pairs={{1,0},{2,1},{3,2},{0,3},{5,4},{6,5},{7,6},{4,7},{9,8},{10,9},{11,1... | collective-permute-start | bytes 1179656 | tf_op jit(solution)/shard_map/while/body/eval_jaxpr/ppermute | solution.py:170
  158.1 75.7 %all-gather.28.cloned.1.call-start = ((), (), s32[]{:S(2)}) async-start(), calls=%async_computation.16 | async-start | bytes 1966080 | tf_op jit(solution)/shard_map/while/body/eval_jaxpr/all_gather | solution.py:191
  197.8 81.8 %reduce-scatter.22.cloned.1.call-start = ((), (), s32[]{:S(2)}) async-start(), calls=%async_computation.17 | async-start | bytes 1966080 | tf_op jit(solution)/shard_map/while/body/eval_jaxpr/reduce_scatter | solution.py:199
  245.2 75.5 %all-gather.30.cloned.1.call-start = ((), (), s32[]{:S(2)}) async-start(), calls=%async_computation.18 | async-start | bytes 1966080 | tf_op jit(solution)/shard_map/while/body/eval_jaxpr/all_gather | solution.py:208
  284.6 122.5 %reduce-scatter.24.cloned.1.call-start = ((), (), s32[]{:S(2)}) async-start(), calls=%async_computation.19 | async-start | bytes 1966080 | tf_op jit(solution)/shard_map/while/body/eval_jaxpr/reduce_scatter | solution.py:262
  409.2 38.3 %all-gather.22.cloned.1.call-start = ((), (), s32[]{:S(2)}) async-start(), calls=%async_computation.11 | async-start | bytes 1966080 | tf_op jit(solution)/shard_map/while/body/eval_jaxpr/all_gather | solution.py:125
  411.1 90.8 %reduce-scatter.18.cloned.1.call-start = ((), (), s32[]{:S(2)}) async-start(), calls=%async_computation.12 | async-start | bytes 1966080 | tf_op jit(solution)/shard_map/while/body/eval_jaxpr/reduce_scatter | solution.py:152
  467.4 56.7 %all-gather.24.cloned.1.call-start = ((), (), s32[]{:S(2)}) async-start(), calls=%async_computation.13 | async-start | bytes 2654208 | tf_op jit(solution)/shard_map/while/body/eval_jaxpr/all_gather | solution.py:114
  468.0 80.5 %all-gather.26.cloned.1.call-start = ((), (), s32[]{:S(2)}) async-start(), calls=%async_computation.14 | async-start | bytes 1327104 | tf_op jit(solution)/shard_map/while/body/eval_jaxpr/all_gather | solution.py:115
  505.9 80.8 %reduce-scatter.20.cloned.1.call-start = ((), (), s32[]{:S(2)}) async-start(), calls=%async_computation.15 | async-start | bytes 1966080 | tf_op jit(solution)/shard_map/while/body/eval_jaxpr/reduce_scatter | solution.py:179
  505.9 21.8 %collective-permute-start = (bf16[256,768]{1,0:T(8,128)(2,1)S(1)}, bf16[256,768]{1,0:T(8,128)(2,1)S(1)}, u32[]{:S(2)}, u32[]{:S(2)}) collective-permute-start(bf16[256,768]{1,0:T(8,128)(2,1)S(1)} %fusion.188), channel_id=1, source_target_pairs={{1,0},{2,1},{3,2},{0,3},{5,4},{6,5},{7,6},{4,7},{9,8},{10,9},{11,1... | collective-permute-start | bytes 1179656 | tf_op jit(solution)/shard_map/while/body/eval_jaxpr/ppermute | solution.py:170
  553.0 75.7 %all-gather.28.cloned.1.call-start = ((), (), s32[]{:S(2)}) async-start(), calls=%async_computation.16 | async-start | bytes 1966080 | tf_op jit(solution)/shard_map/while/body/eval_jaxpr/all_gather | solution.py:191
  592.7 81.8 %reduce-scatter.22.cloned.1.call-start = ((), (), s32[]{:S(2)}) async-start(), calls=%async_computation.17 | async-start | bytes 1966080 | tf_op jit(solution)/shard_map/while/body/eval_jaxpr/reduce_scatter | solution.py:199
  640.0 75.5 %all-gather.30.cloned.1.call-start = ((), (), s32[]{:S(2)}) async-start(), calls=%async_computation.18 | async-start | bytes 1966080 | tf_op jit(solution)/shard_map/while/body/eval_jaxpr/all_gather | solution.py:208
  679.4 122.7 %reduce-scatter.24.cloned.1.call-start = ((), (), s32[]{:S(2)}) async-start(), calls=%async_computation.19 | async-start | bytes 1966080 | tf_op jit(solution)/shard_map/while/body/eval_jaxpr/reduce_scatter | solution.py:262
  809.0 57.6 %reduce-scatter.16.cloned.1.call-start = ((), (), s32[]{:S(2)}) async-start(), calls=%async_computation.9 | async-start | bytes 884736
  811.3 125.8 %all-reduce.6.cloned.1.call-start = ((), (), s32[]{:S(2)}) async-start(), calls=%async_computation.10 | async-start | bytes 9437184
  819.5 163.7 %reduce-scatter.12.cloned.1.call-start = ((), (), s32[]{:S(2)}) async-start(), calls=%async_computation.7 | async-start | bytes 2654208 | tf_op jit(solution)/shard_map/reduce_scatter | solution.py:293
  822.8 206.5 %reduce-scatter.14.cloned.1.call-start = ((), (), s32[]{:S(2)}) async-start(), calls=%async_computation.8 | async-start | bytes 2654208 | tf_op jit(solution)/shard_map/reduce_scatter | solution.py:296
  (126 other events, 1678.7 us)
Sparse Core Ops, SparseCore 0:
  12.9 39.6 all-gather.21
  72.7 34.3 reduce-scatter.17
  158.3 33.5 reduce-scatter.19
  197.9 35.8 all-gather.27
  245.3 34.2 reduce-scatter.21
  284.7 35.8 all-gather.29
  372.7 34.2 reduce-scatter.23
  411.6 35.8 all-gather.21
  467.6 34.3 reduce-scatter.17
  553.1 33.5 reduce-scatter.19
  592.8 35.8 all-gather.27
  640.1 34.2 reduce-scatter.21
  679.6 35.8 all-gather.29
  767.8 34.3 reduce-scatter.23
Sparse Core Ops, SparseCore 1:
  74.9 27.7 all-gather.23
  111.1 25.0 all-gather.25
  469.8 27.6 all-gather.23
  505.9 25.0 all-gather.25
  812.9 33.9 reduce-scatter.15
  850.2 86.9 all-reduce.5
  940.9 42.2 reduce-scatter.11
  987.0 42.1 reduce-scatter.13
